TPU v7x, 128 devices: a whole 4x4x4 slice. The times are simulated.
128 devices in a mesh: heads: 8 (over z, core), width: 4 (over y), sae: 4 (over x).
Axes of the slice: x: 4, y: 4, z: 4, core: 2. Of those that a mesh axis runs over, the one named last changes fastest.
Arguments:
- x_in: bfloat16 [512, 4608], P(None, 'width'), may hold values from -64 to 64
- doc_lengths: int32 [4], replicated, may hold values from 1 to 256, 512 in all
- attn_gain: float32 [4608], P('width'), may hold values from 0.25 to 1.75
- w_query: bfloat16 [4608, 4096], P('width', 'heads'), may hold values from -0.09375 to 0.09375
- w_key: bfloat16 [4608, 2048], P('width', 'heads'), may hold values from -0.09375 to 0.09375
- w_value: bfloat16 [4608, 2048], P('width', 'heads'), may hold values from -0.09375 to 0.09375
- w_out: bfloat16 [4096, 4608], P('heads', 'width'), may hold values from -0.09375 to 0.09375
- post_gain: float32 [4608], replicated, may hold values from 0.25 to 1.75
- enc_weight: bfloat16 [4608, 65536], P(None, ('heads', 'width', 'sae')), may hold values from -0.09375 to 0.09375
- enc_bias: float32 [65536], P(('heads', 'width', 'sae')), may hold values from -1.5 to 0.5
- dec_weight: bfloat16 [65536, 4608], P(('heads', 'width', 'sae')), may hold values from -1 to 1
- dec_bias: float32 [4608], replicated, may hold values from -5 to 5
Outputs:
- grad_enc: bfloat16 [4608, 65536], P(None, ('heads', 'width', 'sae'))
- grad_dec: bfloat16 [65536, 4608], P(('heads', 'width', 'sae'))
- total_loss: float32 [], replicated
Inputs may be any that keep to these rules, and one draw needn't show every extreme that they name: `doc_lengths`: lengths of the 4 documents packed in order; they sum to 512.
All inputs are finite; a program needn't handle non-finite values.
Results may differ from a plain program's by a relative error of at most 0.02.
Values may be sent and summed in bfloat16 or wider, within the bound.
A program may use at most 128 MiB of HBM per device.

v0:
```python
import jax
import jax.numpy as jnp
from jax import lax
from jax.sharding import PartitionSpec as P

D = 4608
HEADS = 32
HEAD_DIM = 128
norm_eps = 1e-06
soft_cap = 50.0
rope_base = 10000.0
l1_weight = 3.0


def rotary(values, position):
    half_dim = values.shape[-1] // 2
    frequency = rope_base ** (-2.0 * jnp.arange(half_dim, dtype=jnp.float32) / values.shape[-1])
    angles = position.astype(jnp.float32)[:, None] * frequency[None, :]
    cosine_table = jnp.cos(angles)[:, None, :]
    sine_table = jnp.sin(angles)[:, None, :]
    first_half = values[..., :half_dim]
    second_half = values[..., half_dim:]
    return jnp.concatenate(
        [
            first_half * cosine_table - second_half * sine_table,
            second_half * cosine_table + first_half * sine_table,
        ],
        axis=-1,
    )


def attend_rows(query_rows, key_rows, value_rows, allowed_rows, scale):
    scores = (
        jnp.einsum("tkgd,skd->kgts", query_rows, key_rows, preferred_element_type=jnp.float32)
        * scale
    )
    capped = soft_cap * jnp.tanh(scores / soft_cap)
    weights = jnp.where(allowed_rows[None, None], jnp.exp(capped), 0.0)
    totals = jnp.sum(weights, axis=-1, keepdims=True)
    probs_bf = (weights / totals).astype(jnp.bfloat16)
    return jnp.einsum(
        "kgts,skd->tkgd", probs_bf, value_rows, preferred_element_type=jnp.float32
    ).astype(jnp.bfloat16)


def per_device(
    x_in,
    doc_lengths,
    attn_gain,
    w_query,
    w_key,
    w_value,
    w_out,
    post_gain,
    enc_weight,
    enc_bias,
    dec_weight,
    dec_bias,
):
    tokens = x_in.shape[0]
    query_heads = w_query.shape[1] // HEAD_DIM
    value_heads = w_key.shape[1] // HEAD_DIM
    boundary = jnp.cumsum(doc_lengths)
    position = jnp.arange(tokens, dtype=jnp.int32)
    segment = jnp.sum((boundary[None, :] <= position[:, None]).astype(jnp.int32), axis=1)
    allowed = (segment[:, None] == segment[None, :]) & (position[None, :] <= position[:, None])
    x_float = x_in.astype(jnp.float32)
    scaled = (x_float * attn_gain).astype(jnp.bfloat16)
    query_part = jnp.dot(scaled, w_query, preferred_element_type=jnp.float32)
    key_part = jnp.dot(scaled, w_key, preferred_element_type=jnp.float32)
    value_part = jnp.dot(scaled, w_value, preferred_element_type=jnp.float32)
    square_part = jnp.sum(x_float * x_float, axis=1)
    query_raw, key_raw, value_raw, square_sums = lax.psum(
        (query_part, key_part, value_part, square_part), "width"
    )
    inverse_rms = lax.rsqrt(square_sums / D + norm_eps)
    query = rotary(
        (query_raw * inverse_rms[:, None]).reshape(tokens, query_heads, HEAD_DIM), position
    ).astype(jnp.bfloat16)
    key_rows = rotary(
        (key_raw * inverse_rms[:, None]).reshape(tokens, value_heads, HEAD_DIM), position
    ).astype(jnp.bfloat16)
    value_rows = (
        (value_raw * inverse_rms[:, None])
        .reshape(tokens, value_heads, HEAD_DIM)
        .astype(jnp.bfloat16)
    )
    query4 = query.reshape(tokens, value_heads, query_heads // value_heads, HEAD_DIM)
    pieces_out = attend_rows(query4, key_rows, value_rows, allowed, (D // HEADS) ** (-0.5))
    mixed = pieces_out.reshape(tokens, query_heads * HEAD_DIM)
    proj_part = jnp.dot(mixed, w_out, preferred_element_type=jnp.float32)
    attn_sum = lax.psum(proj_part, "heads")
    attn_local = attn_sum.astype(jnp.bfloat16)
    attn_proj, x_full = (
        lax.all_gather(attn_local, "width", axis=1, tiled=True),
        lax.all_gather(x_in, "width", axis=1, tiled=True),
    )
    proj_float = attn_proj.astype(jnp.float32)
    inverse_post = lax.rsqrt(jnp.sum(proj_float * proj_float, axis=1) / D + norm_eps)
    resid = (x_full.astype(jnp.float32) + proj_float * inverse_post[:, None] * post_gain).astype(
        jnp.bfloat16
    )
    centered = (resid.astype(jnp.float32) - dec_bias).astype(jnp.bfloat16)
    pre_acts = jnp.dot(centered, enc_weight, preferred_element_type=jnp.float32) + enc_bias
    latent_acts = jnp.maximum(pre_acts, 0.0).astype(jnp.bfloat16)
    row_norms = jnp.sqrt(jnp.sum(jnp.square(dec_weight.astype(jnp.float32)), axis=1) + norm_eps)
    act_sums = jnp.sum(latent_acts.astype(jnp.float32), axis=0)
    penalty_part = jnp.sum(act_sums * row_norms)
    recon_part = jnp.dot(latent_acts, dec_weight, preferred_element_type=jnp.float32)
    recon = lax.psum(recon_part, ("heads", "width", "sae")) + dec_bias
    error = recon - resid.astype(jnp.float32)
    squares_total = jnp.sum(error * error)
    penalty_total = lax.psum(penalty_part, ("heads", "width", "sae"))
    grad_recon = (2.0 / tokens * error).astype(jnp.bfloat16)
    total_loss = (squares_total + l1_weight * penalty_total) / (tokens * D)
    upstream = lax.dot_general(
        grad_recon, dec_weight, (((1,), (1,)), ((), ())), preferred_element_type=jnp.float32
    )
    grad_pre = jnp.where(pre_acts > 0, upstream + l1_weight * row_norms / tokens, 0.0).astype(
        jnp.bfloat16
    )
    grad_enc = lax.dot_general(
        centered, grad_pre, (((0,), (0,)), ((), ())), preferred_element_type=jnp.float32
    ).astype(jnp.bfloat16)
    decoder_term = lax.dot_general(
        latent_acts, grad_recon, (((0,), (0,)), ((), ())), preferred_element_type=jnp.float32
    )
    grad_dec = (
        decoder_term
        + l1_weight
        / tokens
        * act_sums[:, None]
        * dec_weight.astype(jnp.float32)
        / row_norms[:, None]
    ).astype(jnp.bfloat16)
    return (grad_enc, grad_dec, total_loss)


def solution(mesh):
    placed = (
        P(None, "width"),
        P(),
        P("width"),
        P("width", "heads"),
        P("width", "heads"),
        P("width", "heads"),
        P("heads", "width"),
        P(),
        P(None, ("heads", "width", "sae")),
        P(("heads", "width", "sae")),
        P(("heads", "width", "sae"), None),
        P(),
    )
    return jax.shard_map(
        per_device,
        mesh=mesh,
        in_specs=placed,
        out_specs=(P(None, ("heads", "width", "sae")), P(("heads", "width", "sae"), None), P()),
        check_vma=False,
    )
```

profile of v0, /device:TPU:1, one launch (start us, length us, event | category | flops | bytes accessed | tf_op | source)
XLA Modules:
  0.0 471.6 jit_solution(9375944868353371698)
XLA Ops:
  7.3 3.6 fusion.23
  10.9 2.7 fusion.25
  13.6 1.3 fusion.27
  15.5 9.5 %psum.50 = f32[512]{0:T(512)S(1)} all-reduce(f32[512]{0:T(512)S(1)} %fusion.14), channel_id=1, replica_groups=mesh['heads'=8,'width'=4,'sae'=4] {'width'}, use_global_device_ids=true, to_apply=%region_2.3 | all-reduce | flops 512 | bytes 4096 | tf_op jit(solution)/shard_map/psum | solution.py:73
  25.2 0.9 fusion.22
  26.1 1.7 multiply_cosine_fusion
  27.8 49.0 %all-reduce.7.cloned.1.call-done = (f32[512,256]{1,0:T(8,128)}, f32[512,512]{1,0:T(8,128)}, f32[512,256]{1,0:T(8,128)}) async-done(((f32[512,256]{1,0:T(8,128)}, f32[512,512]{1,0:T(8,128)}, f32[512,256]{1,0:T(8,128)}), (f32[512,256]{1,0:T(8,128)}, f32[512,512]{1,0:T(8,128)}, f32[512,256]{1,0:T(8,128)})) %all-reduce.7.cloned.1.call-update) | async-done | bytes 2097168 | tf_op jit(solution)/shard_map/psum | solution.py:73
  76.9 2.1 broadcast_multiply_fusion.1
  79.2 1.5 fusion.40
  80.7 1.4 broadcast_multiply_fusion
  82.1 0.4 reshape.169
  82.5 1.8 subtract_convert_fusion
  84.6 1.3 subtract_convert_fusion.1
  85.9 2.9 fusion.12
  88.8 1.6 fusion.21
  90.4 0.9 fusion.41
  91.3 52.5 %all-reduce.8 = bf16[512,1152]{1,0:T(8,128)(2,1)} all-reduce(f32[512,1152]{1,0:T(8,128)S(1)} %fusion.41), channel_id=1, replica_groups=mesh['heads'=8,'width'=4,'sae'=4] {'heads'}, use_global_device_ids=true, to_apply=%region_8.9 | all-reduce | flops 589824 | bytes 3538944 | tf_op jit(solution)/shard_map/psum | solution.py:92
  143.8 0.7 all-gather.3.cloned.1.call-update
  144.8 51.8 %all-gather.5.cloned.1.call-done = bf16[512,4608]{1,0:T(8,128)(2,1)} async-done(((bf16[512,1152]{1,0:T(8,128)(2,1)}), bf16[512,4608]{1,0:T(8,128)(2,1)}) %all-gather.5.cloned.1.call-update) | async-done | bytes 4718608 | tf_op jit(solution)/shard_map/all_gather | solution.py:95
  196.6 3.3 fusion
  200.0 51.3 %all-gather.3.cloned.1.call-done = bf16[512,4608]{1,0:T(8,128)(2,1)} async-done(((bf16[512,1152]{1,0:T(8,128)(2,1)}), bf16[512,4608]{1,0:T(8,128)(2,1)}) %all-gather.3.cloned.1.call-update) | async-done | bytes 4718608 | tf_op jit(solution)/shard_map/all_gather | solution.py:96
  251.3 5.9 %fusion.3 = bf16[512,4608]{1,0:T(8,128)(2,1)S(1)} fusion(bf16[512,4608]{1,0:T(8,128)(2,1)} %all-gather.5.cloned.1.call-done, bf16[512,4608]{1,0:T(8,128)(2,1)} %all-gather.3.cloned.1.call-done, f32[4608]{0:T(1024)S(1)} %copy-done.8, f32[512]{0:T(512)S(1)} %add_rsqrt_fusion), kind=kLoop, calls=%fused_computation.9 | loop fusion | flops 14155776 | bytes 14176256 | tf_op jit(solution)/shard_map/convert_element_type | solution.py:100
  257.3 6.4 %convert_reduce_fusion = (f32[512]{0:T(512)S(1)}, f32[512,512]{1,0:T(8,128)S(1)}) fusion(f32[512]{0:T(512)S(1)} %copy-done.12, bf16[4608,512]{1,0:T(8,128)(2,1)} %param.20, bf16[512,4608]{1,0:T(8,128)(2,1)S(1)} %fusion.3, f32[4608]{0:T(1024)S(1)} %copy-done.9), kind=kOutput, calls=%fused_computation.32 | convolution fusion | flops 2424045056 | bytes 10508288 | tf_op jit(solution)/shard_map/dot_general | solution.py:104
  263.7 5.1 %fusion.39 = f32[512,4608]{1,0:T(8,128)} fusion(bf16[512,4608]{1,0:T(8,128)(2,1)S(1)} %bitcast.41, f32[512,512]{1,0:T(8,128)S(1)} %get-tuple-element.25), kind=kOutput, calls=%fused_computation.69 | convolution fusion | flops 2416443392 | bytes 15204352 | tf_op jit(solution)/shard_map/dot_general | solution.py:109
  268.8 3.3 fusion.5
  272.2 0.6 multiply_reduce_fusion.1
  272.8 65.8 %psum.55 = f32[]{:T(128)} all-reduce(f32[]{:T(128)} %get-tuple-element.16), channel_id=1, replica_groups=mesh['heads'=8,'width'=4,'sae'=4] {'heads','width','sae'}, use_global_device_ids=true, to_apply=%region_15.16 | all-reduce | flops 1 | bytes 8 | tf_op jit(solution)/shard_map/psum | solution.py:113
  339.2 94.4 %all-reduce.5.cloned.1.call-done = f32[512,4608]{1,0:T(8,128)} async-done(((f32[512,4608]{1,0:T(8,128)}), f32[512,4608]{1,0:T(8,128)}) %all-reduce.5.cloned.1.call-update) | async-done | bytes 9437200 | tf_op jit(solution)/shard_map/psum | solution.py:110
  433.6 8.4 %multiply_reduce_fusion = (f32[]{:T(128)}, bf16[512,4608]{1,0:T(8,128)(2,1)S(1)}) fusion(bf16[512,4608]{1,0:T(8,128)(2,1)} %copy-done.2, f32[512,4608]{1,0:T(8,128)} %all-reduce.5.cloned.1.call-done, f32[4608]{0:T(1024)S(1)} %copy-done.9), kind=kLoop, calls=%fused_computation.15 | loop fusion | flops 16515071 | bytes 18892804 | tf_op jit(solution)/shard_map/reduce_sum | solution.py:112
  442.0 6.7 %fusion.20 = bf16[512,512]{1,0:T(8,128)(2,1)S(1)} fusion(bf16[512,4608]{1,0:T(8,128)(2,1)S(1)} %get-tuple-element.7, bf16[512,4608]{1,0:T(8,128)(2,1)} %param.22, f32[512,512]{1,0:T(8,128)S(1)} %get-tuple-element.25, f32[512]{0:T(512)S(1)} %get-tuple-element.17), kind=kOutput, calls=%fused_computation.30 | convolution fusion | flops 2416967680 | bytes 11012096 | tf_op jit(solution)/shard_map/dot_general | solution.py:116
  448.7 6.8 %convolution_convert_fusion = bf16[4608,512]{1,0:T(8,128)(2,1)} fusion(bf16[512,512]{1,0:T(8,128)(2,1)S(1)} %fusion.20, bf16[512,4608]{1,0:T(8,128)(2,1)} %copy-done.2, f32[4608]{0:T(1024)S(1)} %copy-done.9), kind=kOutput, calls=%fused_computation.17 | convolution fusion | flops 2425356288 | bytes 9979904 | tf_op jit(solution)/shard_map/dot_general | solution.py:122
  456.1 7.8 %fusion.8 = bf16[512,4608]{1,0:T(8,128)(2,1)} fusion(bf16[512,4608]{1,0:T(8,128)(2,1)} %param.22, bf16[512,4608]{1,0:T(8,128)(2,1)} %copy-done.4, f32[512]{0:T(512)S(1)} %get-tuple-element.18, f32[512]{0:T(512)S(1)} %get-tuple-element.19, f32[512,512]{1,0:T(8,128)S(1)} %get-tuple-element.25), kind=kOutput, calls=%fused_computation.14 | convolution fusion | flops 2428239872 | bytes 15208448 | tf_op jit(solution)/shard_map/dot_general | solution.py:125
  (51 shorter events, 1.6 us)
Async XLA Ops:
  7.2 83.3 %copy-start = (bf16[512,1152]{1,0:T(8,128)(2,1)S(1)}, bf16[512,1152]{1,0:T(8,128)(2,1)}, u32[]{:S(2)}) copy-start(bf16[512,1152]{1,0:T(8,128)(2,1)} %param.18) | copy-start | bytes 3538948
  7.2 6.5 %copy-start.3 = (bf16[512,1152]{1,0:T(8,128)(2,1)S(1)}, bf16[512,1152]{1,0:T(8,128)(2,1)}, u32[]{:S(2)}) copy-start(bf16[512,1152]{1,0:T(8,128)(2,1)} %param.12) | copy-start | bytes 3538948
  7.2 6.4 %copy-start.11 = (f32[1152]{0:T(1024)S(1)}, f32[1152]{0:T(1024)}, u32[]{:S(2)}) copy-start(f32[1152]{0:T(1024)} %param.14) | copy-start | bytes 13828
  7.2 6.4 %copy-start.10 = (bf16[1152,256]{1,0:T(8,128)(2,1)S(1)}, bf16[1152,256]{1,0:T(8,128)(2,1)}, u32[]{:S(2)}) copy-start(bf16[1152,256]{1,0:T(8,128)(2,1)} %param.17) | copy-start | bytes 1769476
  7.2 7.8 %copy-start.13 = (s32[4]{0:T(128)S(1)}, s32[4]{0:T(128)}, u32[]{:S(2)}) copy-start(s32[4]{0:T(128)} %param.13) | copy-start | bytes 52
  7.2 69.6 %all-reduce.7.cloned.1.call-start = ((), (), s32[]{:S(2)}) async-start(), calls=%async_computation.3 | async-start | bytes 4194304 | tf_op jit(solution)/shard_map/psum | solution.py:73
  15.0 181.6 %all-gather.5.cloned.1.call-start = ((), (), s32[]{:S(2)}) async-start(), calls=%async_computation.1 | async-start | bytes 5898240 | tf_op jit(solution)/shard_map/all_gather | solution.py:95
  82.4 2.0 copy-start.6
  82.4 2.1 copy-start.5
  85.9 2.9 copy-start.7
  91.3 160.0 %copy-start.8 = (f32[4608]{0:T(1024)S(1)}, f32[4608]{0:T(1024)}, u32[]{:S(2)}) copy-start(f32[4608]{0:T(1024)} %param.19) | copy-start | bytes 55300
  143.8 107.5 %all-gather.3.cloned.1.call-start = ((), (), s32[]{:S(2)}) async-start(), calls=%async_computation | async-start | bytes 5898240 | tf_op jit(solution)/shard_map/all_gather | solution.py:96
  144.5 289.1 %all-reduce.5.cloned.1.call-start = ((), (), s32[]{:S(2)}) async-start(), calls=%async_computation.2 | async-start | bytes 18874368 | tf_op jit(solution)/shard_map/psum | solution.py:110
  199.9 57.3 %copy-start.9 = (f32[4608]{0:T(1024)S(1)}, f32[4608]{0:T(1024)}, u32[]{:S(2)}) copy-start(f32[4608]{0:T(1024)} %param.23) | copy-start | bytes 55300
  199.9 57.3 %copy-start.12 = (f32[512]{0:T(512)S(1)}, f32[512]{0:T(512)}, u32[]{:S(2)}) copy-start(f32[512]{0:T(512)} %param.21) | copy-start | bytes 6148
  251.3 12.4 %slice-start = ((s8[4718592]{0:T(1024)(128)(4,1)}), s8[4194304]{0:T(1024)(128)(4,1)S(1)}, s32[]{:S(2)}) async-start(s8[4718592]{0:T(1024)(128)(4,1)} %bitcast.40), calls=%async_computation.4 | async-start | bytes 8388608
  257.2 6.4 %copy-start.2 = (bf16[512,4608]{1,0:T(8,128)(2,1)}, bf16[512,4608]{1,0:T(8,128)(2,1)S(1)}, u32[]{:S(2)}) copy-start(bf16[512,4608]{1,0:T(8,128)(2,1)S(1)} %fusion.3) | copy-start | bytes 14155780
  257.2 6.5 %slice-start.1 = ((s8[4718592]{0:T(1024)(128)(4,1)}), s8[524288]{0:T(1024)(128)(4,1)S(1)}, s32[]{:S(2)}) async-start(s8[4718592]{0:T(1024)(128)(4,1)} %bitcast.40), calls=%async_computation.5 | async-start | bytes 1048576
  442.0 6.7 %copy-start.4 = (bf16[512,4608]{1,0:T(8,128)(2,1)}, bf16[512,4608]{1,0:T(8,128)(2,1)S(1)}, u32[]{:S(2)}) copy-start(bf16[512,4608]{1,0:T(8,128)(2,1)S(1)} %get-tuple-element.7) | copy-start | bytes 14155780
  456.1 7.9 %copy-start.1 = (bf16[512,1152]{1,0:T(8,128)(2,1)S(1)}, bf16[512,1152]{1,0:T(8,128)(2,1)}, u32[]{:S(2)}) copy-start(bf16[512,1152]{1,0:T(8,128)(2,1)} %param.18) | copy-start | bytes 3538948
Sparse Core Ops, SparseCore 0:
  15.1 61.7 all-reduce.6
  143.9 52.6 all-gather.4
  198.3 52.9 all-gather.2
  268.9 164.6 all-reduce.4
where the time goes:
time: 472 us
  waiting for transfers between devices  247 us (52%)
  blocking collectives  128 us (27%)
  matrix products  45.7 us (10%)
  other arithmetic  31.4 us (7%)
  between operations  16.5 us (3%)
    psum x1, waiting for transfers between devices, per_device(): recon = lax.psum(recon_part, ('heads', 'width', 'sae')) + dec_bias  94.4 us
    psum x1, blocking collectives, per_device(): penalty_total = lax.psum(penalty_part, ('heads', 'width', 'sae'))  65.8 us
    psum x1, blocking collectives, per_device(): attn_sum = lax.psum(proj_part, 'heads')  52.5 us
    all_gather x1, waiting for transfers between devices, per_device(): lax.all_gather(attn_local, 'width', axis=1, tiled=True)  51.8 us
    all_gather x1, waiting for transfers between devices, per_device(): lax.all_gather(x_in, 'width', axis=1, tiled=True)  51.3 us
    psum x1, waiting for transfers between devices, per_device(): lax.psum((query_part, key_part, value_part, square_part), 'width')  49 us
    psum x1, blocking collectives, per_device(): lax.psum((query_part, key_part, value_part, square_part), 'width')  9.54 us
  transfers between devices with their start and end apart: 4, of which 4 were waited for; matrix products, arithmetic and copies ran while one was open for 2% of the time, Pallas kernels for 0%

commit v1 on v0

--- a/solution.py
+++ b/solution.py
@@ -92,7 +92,9 @@
     attn_sum = lax.psum(proj_part, "heads")
     attn_local = attn_sum.astype(jnp.bfloat16)
     attn_proj, x_full = (
-        lax.all_gather(attn_local, "width", axis=1, tiled=True),
+        jnp.concatenate(
+            lax.all_to_all(jnp.stack([attn_local] * lax.axis_size("width")), "width", 0, 0), axis=1
+        ),
         lax.all_gather(x_in, "width", axis=1, tiled=True),
     )
     proj_float = attn_proj.astype(jnp.float32)

time: 472 us -> 430 us (0.911)
  waiting for transfers between devices: 247 us -> 142 us
  blocking collectives: 128 us -> 186 us
  local copies, waits for them, and re-layouts: 2.52 us -> 7.77 us
    all_to_all x0 -> x1, blocking collectives: none -> 53.3 us  [per_device(): lax.all_to_all(jnp.stack([attn_local] * lax.axis_size('width')), 'width',...]
    all_gather x1 -> x0, waiting for transfers between devices: 51.8 us -> none  [per_device(): lax.all_gather(attn_local, 'width', axis=1, tiled=True)]
    all_gather x1, waiting for transfers between devices: 51.3 us -> 0.02 us  [per_device(): lax.all_gather(x_in, 'width', axis=1, tiled=True)]
    convert_element_type x0 -> x1, local copies, waits for them, and re-layouts: none -> 4.9 us  [per_device(): proj_float = attn_proj.astype(jnp.float32)]
  transfers between devices with their start and end apart: 4 -> 3, of which waited for: 4 -> 2; matrix products, arithmetic and copies ran while one was open for 2% -> 7% of each run, Pallas kernels for 0% -> 0%
where the time goes in v1:
time: 430 us; the launch traced here: 429 us
  blocking collectives  186 us (43%)
  waiting for transfers between devices  142 us (33%)
  matrix products  45.8 us (11%)
  other arithmetic  30.7 us (7%)
  between operations  16.5 us (4%)
  local copies, waits for them, and re-layouts  7.77 us (2%)
    psum x1, waiting for transfers between devices, per_device(): recon = lax.psum(recon_part, ('heads', 'width', 'sae')) + dec_bias  92.8 us
    psum x1, blocking collectives, per_device(): penalty_total = lax.psum(penalty_part, ('heads', 'width', 'sae'))  69.7 us
    psum x1, blocking collectives, per_device(): attn_sum = lax.psum(proj_part, 'heads')  53.8 us
    all_to_all x1, blocking collectives, per_device(): lax.all_to_all(jnp.stack([attn_local] * lax.axis_size('width')), 'width',...  53.3 us
    psum x1, waiting for transfers between devices, per_device(): lax.psum((query_part, key_part, value_part, square_part), 'width')  48.3 us
    psum x1, blocking collectives, per_device(): lax.psum((query_part, key_part, value_part, square_part), 'width')  9.55 us
  transfers between devices with their start and end apart: 3, of which 2 were waited for; matrix products, arithmetic and copies ran while one was open for 7% of the time, Pallas kernels for 0%

profile of v1, /device:TPU:1, one launch (start us, length us, event | category | flops | bytes accessed | tf_op | source)
XLA Modules:
  0.0 429.2 jit_solution(10197811682209473873)
XLA Ops:
  7.3 3.6 fusion.20
  10.9 2.8 fusion.22
  13.7 1.3 fusion.24
  15.1 0.7 all-gather.2.cloned.1.call-update
  16.2 9.5 %psum.50 = f32[512]{0:T(512)S(1)} all-reduce(f32[512]{0:T(512)S(1)} %fusion.11), channel_id=1, replica_groups=mesh['heads'=8,'width'=4,'sae'=4] {'width'}, use_global_device_ids=true, to_apply=%region_2.3 | all-reduce | flops 512 | bytes 4096 | tf_op jit(solution)/shard_map/psum | solution.py:73
  26.0 0.9 fusion.19
  26.9 1.7 multiply_cosine_fusion
  28.7 48.3 %all-reduce.7.cloned.1.call-done = (f32[512,256]{1,0:T(8,128)}, f32[512,512]{1,0:T(8,128)}, f32[512,256]{1,0:T(8,128)}) async-done(((f32[512,256]{1,0:T(8,128)}, f32[512,512]{1,0:T(8,128)}, f32[512,256]{1,0:T(8,128)}), (f32[512,256]{1,0:T(8,128)}, f32[512,512]{1,0:T(8,128)}, f32[512,256]{1,0:T(8,128)})) %all-reduce.7.cloned.1.call-update) | async-done | bytes 2097168 | tf_op jit(solution)/shard_map/psum | solution.py:73
  76.9 2.1 broadcast_multiply_fusion.1
  79.3 1.5 fusion.37
  80.8 1.4 broadcast_multiply_fusion
  82.6 1.8 subtract_convert_fusion
  84.7 1.3 subtract_convert_fusion.1
  86.0 2.9 fusion.9
  88.9 1.6 fusion.18
  90.5 0.9 fusion.38
  91.4 53.8 %all-reduce.8 = bf16[512,1152]{1,0:T(8,128)(2,1)S(1)} all-reduce(f32[512,1152]{1,0:T(8,128)S(1)} %fusion.38), channel_id=1, replica_groups=mesh['heads'=8,'width'=4,'sae'=4] {'heads'}, use_global_device_ids=true, to_apply=%region_8.9 | all-reduce | flops 589824 | bytes 3538944 | tf_op jit(solution)/shard_map/psum | solution.py:92
  145.6 53.3 %all_to_all.5 = bf16[4,512,1152]{2,1,0:T(8,128)(2,1)S(1)} all-to-all(bf16[4,512,1152]{2,1,0:T(8,128)(2,1)S(1)} %stack.2), channel_id=1, replica_groups=mesh['heads'=8,'width'=4,'sae'=4] {'width'}, dimensions={0} | all-to-all | bytes 9437184 | tf_op jit(solution)/shard_map/all_to_all | solution.py:96
  198.9 0.6 convert_bitcast_fusion
  199.5 4.9 %copy.41 = f32[4,64,8,1152]{3,2,0,1:T(8,128)} copy(f32[4,64,8,1152]{3,2,1,0:T(8,128)S(1)} %convert_bitcast_fusion) | data formatting | bytes 18874368 | tf_op jit(solution)/shard_map/convert_element_type | solution.py:100
  204.4 1.0 fusion.5
  205.5 6.9 %add_convert_fusion = bf16[512,4608]{1,0:T(8,128)(2,1)S(1)} fusion(f32[512,4608]{1,0:T(8,128)} %bitcast.44, bf16[512,4608]{1,0:T(8,128)(2,1)} %all-gather.2.cloned.1.call-done, f32[4608]{0:T(1024)S(1)} %copy-done.9, f32[512]{0:T(512)S(1)} %add_rsqrt_fusion), kind=kLoop, calls=%fused_computation.14 | loop fusion | flops 11796480 | bytes 18894848 | tf_op jit(solution)/shard_map/convert_element_type | solution.py:102
  212.5 6.5 %convert_reduce_fusion = (f32[512]{0:T(512)S(1)}, f32[512,512]{1,0:T(8,128)S(1)}) fusion(f32[512]{0:T(512)S(1)} %copy-done.13, bf16[4608,512]{1,0:T(8,128)(2,1)} %param.20, bf16[512,4608]{1,0:T(8,128)(2,1)S(1)} %add_convert_fusion, f32[4608]{0:T(1024)S(1)} %copy-done.10), kind=kOutput, calls=%fused_computation.30 | convolution fusion | flops 2424045056 | bytes 10508288 | tf_op jit(solution)/shard_map/dot_general | solution.py:106
  219.0 5.1 %fusion.36 = f32[512,4608]{1,0:T(8,128)} fusion(bf16[512,4608]{1,0:T(8,128)(2,1)S(1)} %bitcast.46, f32[512,512]{1,0:T(8,128)S(1)} %get-tuple-element.25), kind=kOutput, calls=%fused_computation.67 | convolution fusion | flops 2416443392 | bytes 15204352 | tf_op jit(solution)/shard_map/dot_general | solution.py:111
  224.1 3.3 fusion.1
  227.4 0.6 multiply_reduce_fusion.1
  228.0 69.7 %psum.55 = f32[]{:T(128)} all-reduce(f32[]{:T(128)} %get-tuple-element.16), channel_id=1, replica_groups=mesh['heads'=8,'width'=4,'sae'=4] {'heads','width','sae'}, use_global_device_ids=true, to_apply=%region_15.16 | all-reduce | flops 1 | bytes 8 | tf_op jit(solution)/shard_map/psum | solution.py:115
  298.4 92.8 %all-reduce.5.cloned.1.call-done = f32[512,4608]{1,0:T(8,128)} async-done(((f32[512,4608]{1,0:T(8,128)}), f32[512,4608]{1,0:T(8,128)}) %all-reduce.5.cloned.1.call-update) | async-done | bytes 9437200 | tf_op jit(solution)/shard_map/psum | solution.py:112
  391.2 8.4 %multiply_reduce_fusion = (f32[]{:T(128)}, bf16[512,4608]{1,0:T(8,128)(2,1)S(1)}) fusion(bf16[512,4608]{1,0:T(8,128)(2,1)} %copy-done.2, f32[512,4608]{1,0:T(8,128)} %all-reduce.5.cloned.1.call-done, f32[4608]{0:T(1024)S(1)} %copy-done.10), kind=kLoop, calls=%fused_computation.12 | loop fusion | flops 16515071 | bytes 18892804 | tf_op jit(solution)/shard_map/reduce_sum | solution.py:114
  399.6 6.7 %fusion.17 = bf16[512,512]{1,0:T(8,128)(2,1)S(1)} fusion(bf16[512,4608]{1,0:T(8,128)(2,1)S(1)} %get-tuple-element.7, bf16[512,4608]{1,0:T(8,128)(2,1)} %param.22, f32[512,512]{1,0:T(8,128)S(1)} %get-tuple-element.25, f32[512]{0:T(512)S(1)} %get-tuple-element.17), kind=kOutput, calls=%fused_computation.28 | convolution fusion | flops 2416967680 | bytes 11012096 | tf_op jit(solution)/shard_map/dot_general | solution.py:118
  406.3 6.7 %convolution_convert_fusion = bf16[4608,512]{1,0:T(8,128)(2,1)} fusion(bf16[512,512]{1,0:T(8,128)(2,1)S(1)} %fusion.17, bf16[512,4608]{1,0:T(8,128)(2,1)} %copy-done.2, f32[4608]{0:T(1024)S(1)} %copy-done.10), kind=kOutput, calls=%fused_computation.15 | convolution fusion | flops 2425356288 | bytes 9979904 | tf_op jit(solution)/shard_map/dot_general | solution.py:124
  413.7 7.8 %fusion.4 = bf16[512,4608]{1,0:T(8,128)(2,1)} fusion(bf16[512,4608]{1,0:T(8,128)(2,1)} %param.22, bf16[512,4608]{1,0:T(8,128)(2,1)} %copy-done.5, f32[512]{0:T(512)S(1)} %get-tuple-element.18, f32[512]{0:T(512)S(1)} %get-tuple-element.19, f32[512,512]{1,0:T(8,128)S(1)} %get-tuple-element.25), kind=kOutput, calls=%fused_computation.10 | convolution fusion | flops 2428239872 | bytes 15208448 | tf_op jit(solution)/shard_map/dot_general | solution.py:127
  (54 shorter events, 2.1 us)
Async XLA Ops:
  7.2 83.4 %copy-start = (bf16[512,1152]{1,0:T(8,128)(2,1)S(1)}, bf16[512,1152]{1,0:T(8,128)(2,1)}, u32[]{:S(2)}) copy-start(bf16[512,1152]{1,0:T(8,128)(2,1)} %param.18) | copy-start | bytes 3538948
  7.2 6.5 %copy-start.3 = (bf16[512,1152]{1,0:T(8,128)(2,1)S(1)}, bf16[512,1152]{1,0:T(8,128)(2,1)}, u32[]{:S(2)}) copy-start(bf16[512,1152]{1,0:T(8,128)(2,1)} %param.12) | copy-start | bytes 3538948
  7.2 6.5 %copy-start.12 = (f32[1152]{0:T(1024)S(1)}, f32[1152]{0:T(1024)}, u32[]{:S(2)}) copy-start(f32[1152]{0:T(1024)} %param.14) | copy-start | bytes 13828
  7.2 69.7 %all-reduce.7.cloned.1.call-start = ((), (), s32[]{:S(2)}) async-start(), calls=%async_computation.3 | async-start | bytes 4194304 | tf_op jit(solution)/shard_map/psum | solution.py:73
  7.3 6.5 %copy-start.11 = (bf16[1152,256]{1,0:T(8,128)(2,1)S(1)}, bf16[1152,256]{1,0:T(8,128)(2,1)}, u32[]{:S(2)}) copy-start(bf16[1152,256]{1,0:T(8,128)(2,1)} %param.17) | copy-start | bytes 1769476
  10.9 5.0 %copy-start.4 = (bf16[512,1152]{1,0:T(8,128)(2,1)S(1)}, bf16[512,1152]{1,0:T(8,128)(2,1)}, u32[]{:S(2)}) copy-start(bf16[512,1152]{1,0:T(8,128)(2,1)} %param.12) | copy-start | bytes 3538948
  10.9 14.9 %copy-start.14 = (s32[4]{0:T(128)S(1)}, s32[4]{0:T(128)}, u32[]{:S(2)}) copy-start(s32[4]{0:T(128)} %param.13) | copy-start | bytes 52
  15.1 190.4 %all-gather.2.cloned.1.call-start = ((), (), s32[]{:S(2)}) async-start(), calls=%async_computation.1 | async-start | bytes 5898240 | tf_op jit(solution)/shard_map/all_gather | solution.py:98
  15.8 375.4 %all-reduce.5.cloned.1.call-start = ((), (), s32[]{:S(2)}) async-start(), calls=%async_computation.2 | async-start | bytes 18874368 | tf_op jit(solution)/shard_map/psum | solution.py:112
  82.5 2.0 copy-start.7
  82.5 2.1 copy-start.6
  86.0 2.9 copy-start.8
  204.4 1.0 copy-start.9
  205.5 7.0 %copy-start.10 = (f32[4608]{0:T(1024)S(1)}, f32[4608]{0:T(1024)}, u32[]{:S(2)}) copy-start(f32[4608]{0:T(1024)} %param.23) | copy-start | bytes 55300
  205.5 7.0 %copy-start.13 = (f32[512]{0:T(512)S(1)}, f32[512]{0:T(512)}, u32[]{:S(2)}) copy-start(f32[512]{0:T(512)} %param.21) | copy-start | bytes 6148
  205.5 13.5 %slice-start = ((s8[4718592]{0:T(1024)(128)(4,1)}), s8[524288]{0:T(1024)(128)(4,1)S(1)}, s32[]{:S(2)}) async-start(s8[4718592]{0:T(1024)(128)(4,1)} %bitcast.45), calls=%async_computation.4 | async-start | bytes 1048576
  212.5 6.5 %copy-start.2 = (bf16[512,4608]{1,0:T(8,128)(2,1)}, bf16[512,4608]{1,0:T(8,128)(2,1)S(1)}, u32[]{:S(2)}) copy-start(bf16[512,4608]{1,0:T(8,128)(2,1)S(1)} %add_convert_fusion) | copy-start | bytes 14155780
  212.5 6.5 %slice-start.1 = ((s8[4718592]{0:T(1024)(128)(4,1)}), s8[4194304]{0:T(1024)(128)(4,1)S(1)}, s32[]{:S(2)}) async-start(s8[4718592]{0:T(1024)(128)(4,1)} %bitcast.45), calls=%async_computation.5 | async-start | bytes 8388608
  399.6 6.7 %copy-start.5 = (bf16[512,4608]{1,0:T(8,128)(2,1)}, bf16[512,4608]{1,0:T(8,128)(2,1)S(1)}, u32[]{:S(2)}) copy-start(bf16[512,4608]{1,0:T(8,128)(2,1)S(1)} %get-tuple-element.7) | copy-start | bytes 14155780
  413.7 7.9 %copy-start.1 = (bf16[512,1152]{1,0:T(8,128)(2,1)S(1)}, bf16[512,1152]{1,0:T(8,128)(2,1)}, u32[]{:S(2)}) copy-start(bf16[512,1152]{1,0:T(8,128)(2,1)} %param.18) | copy-start | bytes 3538948
Sparse Core Ops, SparseCore 0:
  15.2 61.7 all-reduce.6
  78.6 52.3 all-gather.1
  224.2 166.9 all-reduce.4
